TPU v7x, 32 devices: a whole 2x2x4 slice. The times are simulated.
32 devices in a mesh: seq: 8 (over z, y), mp: 4 (over x, core).
Axes of the slice: x: 2, y: 2, z: 4, core: 2. Of those that a mesh axis runs over, the one named last changes fastest.
Arguments:
- incoming_image_patches: bfloat16 [1, 128, 128, 1152], P(None, 'seq', 'mp'), may hold values from -6 to 6
- initial_standardize_scaling: float32 [1152], replicated, may hold values from 0.1 to 1.9
- acceptance_matrix: bfloat16 [1152, 1024], P(None, 'mp'), may hold values from -0.1875 to 0.1875
- addressing_matrix: bfloat16 [1152, 1024], P(None, 'mp'), may hold values from -0.1875 to 0.1875
- content_matrix: bfloat16 [1152, 1024], P(None, 'mp'), may hold values from -0.1875 to 0.1875
- forgetting_lowdim_left_factor: bfloat16 [1152, 64], replicated, may hold values from -0.1875 to 0.1875
- forgetting_lowdim_right_factor: bfloat16 [64, 1024], P(None, 'mp'), may hold values from -1.5 to 1.5
- forgetting_baseline: float32 [1024], P('mp'), may hold values from -6 to 1
- self_token_reward: float32 [1024], P('mp'), may hold values from -3 to 3
- horizontal_cluster_scaling: float32 [1024], P('mp'), may hold values from 0.1 to 1.9
- vertical_cluster_scaling: float32 [1024], P('mp'), may hold values from 0.1 to 1.9
- temporal_mix_projection_matrix: bfloat16 [1024, 1152], P('mp'), may hold values from -0.1875 to 0.1875
- later_standardize_scaling: float32 [1152], replicated, may hold values from 0.1 to 1.9
- feature_mix_addressing_matrix: bfloat16 [1152, 4608], P('seq', 'mp'), may hold values from -0.1875 to 0.1875
- feature_mix_content_matrix: bfloat16 [4608, 1152], P('mp', 'seq'), may hold values from -0.09375 to 0.09375
Outputs:
- block_out: bfloat16 [1, 128, 128, 1152], P(None, 'seq', 'mp')
All inputs are finite; a program needn't handle non-finite values.
Results may differ from a plain program's by a relative error of at most 0.017.
Values may be sent and summed in bfloat16 or wider, within the bound.
A program may use at most 128 MiB of HBM per device.

v0:
```python
import jax
import jax.numpy as jnp
from jax import lax
from jax.sharding import PartitionSpec as P

SUBSPACE_SIZE = 64


def layer_norm(inputs, gain):
    values = inputs.astype(jnp.float32)
    average = jnp.mean(values, axis=-1, keepdims=True)
    centred = values - average
    spread = jnp.mean(centred * centred, axis=-1, keepdims=True)
    return (centred * lax.rsqrt(spread + 1e-05) * gain).astype(jnp.bfloat16)


def heads_first(array, nheads):
    number, length, inner_width = array.shape
    shaped = array.astype(jnp.float32).reshape(number, length, nheads, inner_width // nheads)
    return shaped.transpose(0, 2, 1, 3)


def recurrence(recept_in, keying_in, decays_in, valued_in, boost_in, gain):
    number, length, inner_width = recept_in.shape
    nheads = inner_width // SUBSPACE_SIZE
    head_size = inner_width // nheads
    blocks = length // 16
    acceptance_horizontal_lines = heads_first(recept_in, nheads)
    addressing_horizontal_lines = heads_first(keying_in, nheads)
    decays = heads_first(decays_in, nheads)
    content_horizontal_lines = heads_first(valued_in, nheads)
    boost = boost_in.reshape(nheads, 1, head_size)
    running = jnp.cumsum(decays, axis=2)
    before = running - decays
    before_blocks = before.reshape(number, nheads, blocks, 16, head_size)
    anchor = before_blocks[:, :, :, :1, :]
    queries = acceptance_horizontal_lines.reshape(number, nheads, blocks, 16, head_size) * jnp.exp(
        before_blocks - anchor
    )
    places = jnp.arange(length)
    limits = (jnp.arange(blocks) + 1) * 16
    usable = places[None, :] < limits[:, None]
    exponent = anchor - running[:, :, None, :, :]
    exponent = jnp.where(usable[None, None, :, :, None], exponent, -10000.0)
    weighted = addressing_horizontal_lines[:, :, None, :, :] * jnp.exp(exponent)
    scores = jnp.einsum("nhbqc,nhbsc->nhbqs", queries, weighted, precision=lax.Precision.HIGHEST)
    query_places = places.reshape(blocks, 16)
    earlier = places[None, None, :] < query_places[:, :, None]
    scores = jnp.where(earlier[None, None], scores, 0.0)
    current = jnp.sum(acceptance_horizontal_lines * boost * addressing_horizontal_lines, axis=-1)
    summed = jnp.einsum(
        "nhbqs,nhsc->nhbqc", scores, content_horizontal_lines, precision=lax.Precision.HIGHEST
    )
    summed = (
        summed.reshape(number, nheads, length, head_size)
        + current[..., None] * content_horizontal_lines
    )
    average = jnp.mean(summed, axis=-1, keepdims=True)
    centred = summed - average
    spread = jnp.mean(centred * centred, axis=-1, keepdims=True)
    normed = (
        (centred * lax.rsqrt(spread + 0.00064))
        .transpose(0, 2, 1, 3)
        .reshape(number, length, inner_width)
    )
    return (normed * gain).astype(jnp.bfloat16)


def lines_of_columns(array):
    images, height, columns, inner_width = array.shape
    return jnp.swapaxes(array, 1, 2).reshape(images * columns, height, inner_width)


def shards(
    incoming_image_patches,
    initial_standardize_scaling,
    acceptance_matrix,
    addressing_matrix,
    content_matrix,
    forgetting_lowdim_left_factor,
    forgetting_lowdim_right_factor,
    forgetting_baseline,
    self_token_reward,
    horizontal_cluster_scaling,
    vertical_cluster_scaling,
    temporal_mix_projection_matrix,
    later_standardize_scaling,
    feature_mix_addressing_matrix,
    feature_mix_content_matrix,
):
    images, row_count, part_cols, model_width = incoming_image_patches.shape
    whole_rows = lax.all_gather(incoming_image_patches, "mp", axis=2, tiled=True)
    full_cols = whole_rows.shape[2]
    inner_width = acceptance_matrix.shape[1]
    grid_shape = (images, row_count, full_cols, inner_width)
    xn1 = layer_norm(whole_rows, initial_standardize_scaling).reshape(-1, model_width)
    acceptance_horizontal_lines = jnp.dot(
        xn1, acceptance_matrix, preferred_element_type=jnp.float32
    ).astype(jnp.bfloat16)
    addressing_horizontal_lines = jnp.dot(
        xn1, addressing_matrix, preferred_element_type=jnp.float32
    ).astype(jnp.bfloat16)
    content_horizontal_lines = jnp.dot(
        xn1, content_matrix, preferred_element_type=jnp.float32
    ).astype(jnp.bfloat16)
    latent = jnp.tanh(
        jnp.dot(xn1, forgetting_lowdim_left_factor, preferred_element_type=jnp.float32)
    ).astype(jnp.bfloat16)
    forgetting_log_amount = (
        -0.7
        * jax.nn.sigmoid(
            forgetting_baseline
            + jnp.dot(latent, forgetting_lowdim_right_factor, preferred_element_type=jnp.float32)
        )
    ).astype(jnp.bfloat16)
    recept_grid = acceptance_horizontal_lines.reshape(grid_shape)
    keying_grid = addressing_horizontal_lines.reshape(grid_shape)
    decay_grid = forgetting_log_amount.reshape(grid_shape)
    line_shape = (images * row_count, full_cols, inner_width)
    horizontal_recurrence_result = recurrence(
        acceptance_horizontal_lines.reshape(line_shape),
        addressing_horizontal_lines.reshape(line_shape),
        forgetting_log_amount.reshape(line_shape),
        content_horizontal_lines.reshape(line_shape),
        self_token_reward,
        horizontal_cluster_scaling,
    )
    col_recept, col_keying, col_decay, col_valued = (
        lax.all_to_all(recept_grid, "seq", split_axis=2, concat_axis=1, tiled=True),
        lax.all_to_all(keying_grid, "seq", split_axis=2, concat_axis=1, tiled=True),
        lax.all_to_all(decay_grid, "seq", split_axis=2, concat_axis=1, tiled=True),
        lax.all_to_all(
            horizontal_recurrence_result.reshape(grid_shape),
            "seq",
            split_axis=2,
            concat_axis=1,
            tiled=True,
        ),
    )
    height = col_recept.shape[1]
    columns = col_recept.shape[2]
    vertical_recurrence_result = recurrence(
        lines_of_columns(col_recept),
        lines_of_columns(col_keying),
        lines_of_columns(col_decay),
        lines_of_columns(col_valued),
        self_token_reward,
        vertical_cluster_scaling,
    )
    back_grid = jnp.swapaxes(
        vertical_recurrence_result.reshape(images, columns, height, inner_width), 1, 2
    )
    row_grid = lax.all_to_all(back_grid, "seq", split_axis=1, concat_axis=2, tiled=True)
    partial_value = jnp.dot(
        row_grid.reshape(-1, inner_width),
        temporal_mix_projection_matrix,
        preferred_element_type=jnp.float32,
    )
    partial_value = lax.optimization_barrier(partial_value.astype(jnp.bfloat16)).astype(jnp.float32)
    partial_value = partial_value.reshape(images, row_count, full_cols, model_width)
    totals = lax.psum(partial_value.astype(jnp.bfloat16), "mp").astype(jnp.float32)
    residual_all = (whole_rows.astype(jnp.float32) + totals).astype(jnp.bfloat16)
    mix_input = layer_norm(residual_all, later_standardize_scaling)
    residual = lax.dynamic_slice_in_dim(
        residual_all, lax.axis_index("mp") * part_cols, part_cols, 2
    )
    flattened = mix_input.reshape(-1, model_width)
    hidden_pre = jnp.dot(
        flattened,
        lax.all_gather(feature_mix_addressing_matrix, "seq", axis=0, tiled=True),
        preferred_element_type=jnp.float32,
    )
    positive = jnp.maximum(hidden_pre, 0.0)
    hidden = (positive * positive).astype(jnp.bfloat16)
    downward = jnp.dot(
        hidden,
        lax.all_gather(feature_mix_content_matrix, "seq", axis=1, tiled=True),
        preferred_element_type=jnp.float32,
    )
    downward = lax.optimization_barrier(downward.astype(jnp.bfloat16)).astype(jnp.float32)
    downward = downward.reshape(images, row_count, full_cols, model_width)
    mixed = lax.psum_scatter(
        downward.astype(jnp.bfloat16), "mp", scatter_dimension=2, tiled=True
    ).astype(jnp.float32)
    return (residual.astype(jnp.float32) + mixed).astype(jnp.bfloat16)


def solution(mesh):
    placed = (
        P(None, "seq", "mp", None),
        P(),
        P(None, "mp"),
        P(None, "mp"),
        P(None, "mp"),
        P(),
        P(None, "mp"),
        P("mp"),
        P("mp"),
        P("mp"),
        P("mp"),
        P("mp", None),
        P(),
        P("seq", "mp"),
        P("mp", "seq"),
    )
    return jax.shard_map(
        shards, mesh=mesh, in_specs=placed, out_specs=P(None, "seq", "mp", None), check_vma=False
    )
```

profile of v0, /device:TPU:0, one launch (start us, length us, event | category | flops | bytes accessed | tf_op | source)
XLA Modules:
  0.0 550.7 jit_solution(13070111403937969308)
XLA Ops:
  9.0 40.9 %all-gather.4.cloned.1.call-done = bf16[1,16,128,1152]{3,2,1,0:T(8,128)(2,1)} async-done(((bf16[1,16,32,1152]{3,2,1,0:T(8,128)(2,1)}), bf16[1,16,128,1152]{3,2,1,0:T(8,128)(2,1)}) %all-gather.4.cloned.1.call-update) | async-done | bytes 4718608 | tf_op jit(solution)/shard_map/all_gather | solution.py:92
  49.9 3.2 convert_reduce_fusion
  57.0 2.2 copy-done.9
  60.8 3.1 reshape.301
  63.9 4.9 copy.216
  68.8 4.8 copy.187
  73.7 4.5 fusion.54
  78.1 3.1 reshape.302
  81.3 8.0 %bitcast_subtract_fusion = (f32[16,4,128,64]{3,0,1,2:T(8,128)S(1)}, f32[16,4,128,64]{3,0,1,2:T(8,128)}) fusion(f32[16,128,4,64]{3,2,1,0:T(4,128)} %reshape.302), kind=kOutput, calls=%fused_computation.42 | output fusion | flops 67108864 | bytes 6291456 | tf_op jit(solution)/shard_map/jit(cumsum)/reduce_window_sum | solution.py:33
  91.4 4.8 copy.196
  96.2 3.9 convolution_convert_fusion.3
  101.1 3.7 reshape.303
  104.8 3.5 copy.194
  108.3 5.7 %convolution_convert_fusion.2 = bf16[2048,256]{1,0:T(8,128)(2,1)} fusion(bf16[2048,1152]{1,0:T(8,128)(2,1)} %bitcast.152, bf16[1152,256]{1,0:T(8,128)(2,1)} %param.19), kind=kOutput, calls=%fused_computation.66 | convolution fusion | flops 1208483840 | bytes 6356992 | tf_op jit(solution)/shard_map/dot_general | solution.py:103
  114.1 2.3 copy.197
  117.8 22.1 %fusion.1 = f32[16,4,8,16,128]{4,3,2,1,0:T(8,128)S(1)} fusion(f32[16,4,128,64]{2,3,1,0:T(8,128)} %copy.196, f32[16,4,8,64]{3,2,1,0:T(8,128)S(1)} %copy.191, f32[16,4,128,64]{2,3,1,0:T(8,128)S(1)} %bitcast.135, pred[8,128]{1,0:T(8,128)(4,1)S(1)} %iota_compare_fusion.1, f32[16,4,8,16,64]{4,3,2,1,0:T(8,128)} %bitcast.161, f32[16,4,8,16,64]{4,0,1,3,2:T(8,128)} %bitcast.147), kind=kOutput, calls=%fused_computation.1 | convolution fusion | flops 818937856 | bytes 12715008 | tf_op jit(solution)/shard_map/nhbqc,nhbsc->nhbqs/dot_general | solution.py:46
  140.0 3.9 fusion.44
  143.8 3.2 copy.200
  147.1 2.9 fusion.57
  152.7 2.3 copy.201
  156.3 5.6 %all-to-all-start.3 = ((bf16[1,16,128,256]{3,1,0,2:T(8,128)(2,1)}), bf16[1,16,128,256]{3,1,0,2:T(8,128)(2,1)}, u32[]{:S(2)}, u32[]{:S(2)}) async-start(bf16[1,16,128,256]{3,1,0,2:T(8,128)(2,1)} %multiply_convert_fusion.1), calls=%async_computation.3 | async-start | bytes 2097152 | tf_op jit(solution)/shard_map/all_to_all | solution.py:132
  162.0 2.9 copy.173
  164.8 23.4 %all-to-all-done.3 = bf16[1,16,128,256]{3,1,0,2:T(8,128)(2,1)} async-done(((bf16[1,16,128,256]{3,1,0,2:T(8,128)(2,1)}), bf16[1,16,128,256]{3,1,0,2:T(8,128)(2,1)}, u32[]{:S(2)}, u32[]{:S(2)}) %all-to-all-start.3) | async-done | bytes 1048608 | tf_op jit(solution)/shard_map/all_to_all | solution.py:132
  188.2 4.2 all-to-all-start.1
  194.0 24.0 %all-to-all-done.1 = bf16[1,16,128,256]{3,1,0,2:T(8,128)(2,1)} async-done(((bf16[1,16,128,256]{3,1,0,2:T(8,128)(2,1)}), bf16[1,16,128,256]{3,1,0,2:T(8,128)(2,1)}, u32[]{:S(2)}, u32[]{:S(2)}) %all-to-all-start.1) | async-done | bytes 1048608 | tf_op jit(solution)/shard_map/all_to_all | solution.py:131
  218.1 3.6 all-to-all-start
  223.2 24.2 %all-to-all-done = bf16[1,16,128,256]{3,1,0,2:T(8,128)(2,1)S(1)} async-done(((bf16[1,16,128,256]{3,1,0,2:T(8,128)(2,1)}), bf16[1,16,128,256]{3,1,0,2:T(8,128)(2,1)S(1)}, u32[]{:S(2)}, u32[]{:S(2)}) %all-to-all-start) | async-done | bytes 1048608 | tf_op jit(solution)/shard_map/all_to_all | solution.py:129
  247.5 4.2 all-to-all-start.2
  260.5 4.6 copy.177
  265.1 6.1 %bitcast_subtract_fusion.1 = (f32[16,4,128,64]{3,0,1,2:T(8,128)S(1)}, f32[16,4,128,64]{3,0,1,2:T(8,128)}) fusion(f32[16,128,4,64]{3,0,2,1:T(8,128)} %copy.177), kind=kOutput, calls=%fused_computation.45 | output fusion | flops 67108864 | bytes 6291456 | tf_op jit(solution)/shard_map/jit(cumsum)/reduce_window_sum | solution.py:33
  271.2 2.0 copy-done.7
  273.4 4.7 copy.185
  282.3 2.8 copy.172
  288.5 3.0 copy.183
  291.5 22.4 %fusion.6 = f32[16,4,8,16,128]{4,3,2,1,0:T(8,128)S(1)} fusion(f32[16,4,128,64]{2,3,1,0:T(8,128)} %copy.185, f32[16,4,8,64]{3,2,1,0:T(8,128)S(1)} %copy.178, f32[16,4,128,64]{2,3,1,0:T(8,128)} %bitcast.140, pred[8,128]{1,0:T(8,128)(4,1)S(1)} %iota_compare_fusion.1, f32[16,4,8,16,64]{4,3,2,1,0:T(8,128)} %bitcast.160, f32[16,4,8,16,64]{4,0,1,3,2:T(8,128)} %bitcast.145), kind=kOutput, calls=%fused_computation.6 | convolution fusion | flops 818937856 | bytes 12715008 | tf_op jit(solution)/shard_map/nhbqc,nhbsc->nhbqs/dot_general | solution.py:46
  313.8 3.8 fusion.46
  317.6 4.2 copy.205
  321.8 3.2 fusion.80
  326.0 2.1 copy.210
  330.0 30.6 %all_to_all.69 = bf16[1,128,16,256]{3,2,0,1:T(8,128)(2,1)S(1)} all-to-all(bf16[1,128,16,256]{3,2,0,1:T(8,128)(2,1)S(1)} %fusion.68), channel_id=1, replica_groups=mesh['seq'=8,'mp'=4] {'seq'}, dimensions={1} | all-to-all | bytes 2097152 | tf_op jit(solution)/shard_map/all_to_all | solution.py:153
  360.7 3.7 convolution_convert_fusion.1
  365.7 91.0 %all-reduce.2.cloned.1.call-done = bf16[1,16,128,1152]{3,2,1,0:T(8,128)(2,1)} async-done(((bf16[1,16,128,1152]{3,2,1,0:T(8,128)(2,1)}), bf16[1,16,128,1152]{3,2,1,0:T(8,128)(2,1)}) %all-reduce.2.cloned.1.call-update) | async-done | bytes 4718608 | tf_op jit(solution)/shard_map/psum | solution.py:161
  456.6 5.3 convert_reduce_fusion.1
  464.0 3.2 fusion.21
  467.3 8.3 %all-gather.8.cloned.1.call-done = bf16[1152,1152]{0,1:T(8,128)(2,1)} async-done(((bf16[1152,144]{0,1:T(8,128)(2,1)}), bf16[1152,1152]{0,1:T(8,128)(2,1)}) %all-gather.8.cloned.1.call-update) | async-done | bytes 2654224 | tf_op jit(solution)/shard_map/all_gather | solution.py:177
  475.5 18.4 %convolution_convert_fusion = bf16[2048,1152]{1,0:T(8,128)(2,1)} fusion(bf16[1152,1152]{0,1:T(8,128)(2,1)} %all-gather.8.cloned.1.call-done, bf16[2048,1152]{1,0:T(8,128)(2,1)} %bitcast.153, bf16[1152,1152]{1,0:T(8,128)(2,1)} %all-gather.6.cloned.1.call-done), kind=kOutput, calls=%fused_computation.40 | convolution fusion | flops 10881073152 | bytes 14745600 | tf_op jit(solution)/shard_map/dot_general | solution.py:175
  493.9 46.6 %reduce-scatter.2.cloned.1.call-done = bf16[1,16,32,1152]{3,2,1,0:T(8,128)(2,1)} async-done(((bf16[1,16,128,1152]{3,2,1,0:T(8,128)(2,1)}), bf16[1,16,32,1152]{3,2,1,0:T(8,128)(2,1)}) %reduce-scatter.2.cloned.1.call-update) | async-done | bytes 1179664 | tf_op jit(solution)/shard_map/reduce_scatter | solution.py:182
  540.5 2.9 add_convert_fusion
  (111 shorter events, 41.5 us)
Async XLA Ops:
  7.4 353.3 %copy-start = (bf16[256,1152]{1,0:T(8,128)(2,1)S(1)}, bf16[256,1152]{1,0:T(8,128)(2,1)}, u32[]{:S(2)}) copy-start(bf16[256,1152]{1,0:T(8,128)(2,1)} %param.26) | copy-start | bytes 1769476
  7.4 42.5 %all-gather.4.cloned.1.call-start = ((), (), s32[]{:S(2)}) async-start(), calls=%async_computation.6 | async-start | bytes 5898240 | tf_op jit(solution)/shard_map/all_gather | solution.py:92
  9.0 46.1 %copy-start.17 = (f32[1152]{0:T(1024)S(1)}, f32[1152]{0:T(1024)}, u32[]{:S(2)}) copy-start(f32[1152]{0:T(1024)} %param.16) | copy-start | bytes 13828
  49.9 3.8 copy-start.1
  55.1 4.1 copy-start.21
  57.0 2.2 copy-start.9
  60.8 8.0 %copy-start.10 = (bf16[2048,256]{1,0:T(8,128)(2,1)}, bf16[2048,256]{1,0:T(8,128)(2,1)S(1)}, u32[]{:S(2)}) copy-start(bf16[2048,256]{1,0:T(8,128)(2,1)S(1)} %convolution_convert_fusion.4) | copy-start | bytes 3145732
  68.8 4.8 copy-start.23
  68.8 4.8 copy-start.24
  68.8 4.8 copy-start.25
  78.1 11.1 %copy-start.14 = (bf16[2048,256]{1,0:T(8,128)(2,1)}, bf16[2048,256]{1,0:T(8,128)(2,1)S(1)}, u32[]{:S(2)}) copy-start(bf16[2048,256]{1,0:T(8,128)(2,1)S(1)} %fusion.54) | copy-start | bytes 3145732
  89.3 1.9 copy-start.8
  89.3 7.0 %copy-start.22 = (bf16[1152,256]{1,0:T(8,128)(2,1)S(1)}, bf16[1152,256]{1,0:T(8,128)(2,1)}, u32[]{:S(2)}) copy-start(bf16[1152,256]{1,0:T(8,128)(2,1)} %param.18) | copy-start | bytes 1769476
  100.1 1.0 copy-start.12
  108.3 9.5 %copy-start.6 = (f32[16,128,4,64]{1,3,2,0:T(8,128)}, f32[16,128,4,64]{1,3,2,0:T(8,128)S(1)}, u32[]{:S(2)}) copy-start(f32[16,128,4,64]{1,3,2,0:T(8,128)S(1)} %copy.194) | copy-start | bytes 6291460
  117.8 22.1 %copy-start.3 = (bf16[32,8,16,128]{3,2,1,0:T(8,128)(2,1)}, bf16[32,8,16,128]{3,2,1,0:T(8,128)(2,1)S(1)}, u32[]{:S(2)}) copy-start(bf16[32,8,16,128]{3,2,1,0:T(8,128)(2,1)S(1)} %copy.223) | copy-start | bytes 3145732
  147.1 2.9 copy-start.4
  150.9 4.2 copy-start.19
  156.3 36.2 %copy-start.11 = (bf16[2048,256]{1,0:T(8,128)(2,1)S(1)}, bf16[2048,256]{1,0:T(8,128)(2,1)}, u32[]{:S(2)}) copy-start(bf16[2048,256]{1,0:T(8,128)(2,1)} %copy-done.10) | copy-start | bytes 3145732
  156.3 31.9 %all-to-all-start.3 = ((bf16[1,16,128,256]{3,1,0,2:T(8,128)(2,1)}), bf16[1,16,128,256]{3,1,0,2:T(8,128)(2,1)}, u32[]{:S(2)}, u32[]{:S(2)}) async-start(bf16[1,16,128,256]{3,1,0,2:T(8,128)(2,1)} %multiply_convert_fusion.1), calls=%async_computation.3 | async-start | bytes 2097152 | tf_op jit(solution)/shard_map/all_to_all | solution.py:132
  161.9 59.7 %copy-start.13 = (bf16[2048,256]{1,0:T(8,128)(2,1)S(1)}, bf16[2048,256]{1,0:T(8,128)(2,1)}, u32[]{:S(2)}) copy-start(bf16[2048,256]{1,0:T(8,128)(2,1)} %copy-done.12) | copy-start | bytes 3145732
  188.2 29.8 %all-to-all-start.1 = ((bf16[1,16,128,256]{3,1,0,2:T(8,128)(2,1)}), bf16[1,16,128,256]{3,1,0,2:T(8,128)(2,1)}, u32[]{:S(2)}, u32[]{:S(2)}) async-start(bf16[1,16,128,256]{3,1,0,2:T(8,128)(2,1)} %copy.173), calls=%async_computation.1 | async-start | bytes 2097152 | tf_op jit(solution)/shard_map/all_to_all | solution.py:131
  218.1 29.4 %all-to-all-start = ((bf16[1,16,128,256]{3,1,0,2:T(8,128)(2,1)}), bf16[1,16,128,256]{3,1,0,2:T(8,128)(2,1)S(1)}, u32[]{:S(2)}, u32[]{:S(2)}) async-start(bf16[1,16,128,256]{3,1,0,2:T(8,128)(2,1)} %copy.168), calls=%async_computation | async-start | bytes 2097152 | tf_op jit(solution)/shard_map/all_to_all | solution.py:129
  247.5 7.7 %copy-start.15 = (bf16[1,16,128,256]{3,1,0,2:T(8,128)(2,1)}, bf16[1,16,128,256]{3,1,0,2:T(8,128)(2,1)S(1)}, u32[]{:S(2)}) copy-start(bf16[1,16,128,256]{3,1,0,2:T(8,128)(2,1)S(1)} %all-to-all-done) | copy-start | bytes 3145732
  247.5 37.7 %all-to-all-start.2 = ((bf16[1,16,128,256]{3,1,0,2:T(8,128)(2,1)}), bf16[1,16,128,256]{3,1,0,2:T(8,128)(2,1)}, u32[]{:S(2)}, u32[]{:S(2)}) async-start(bf16[1,16,128,256]{3,1,0,2:T(8,128)(2,1)} %copy.180), calls=%async_computation.2 | async-start | bytes 2097152 | tf_op jit(solution)/shard_map/all_to_all | solution.py:130
  251.7 204.9 %all-reduce.2.cloned.1.call-start = ((), (), s32[]{:S(2)}) async-start(), calls=%async_computation.7 | async-start | bytes 9437184 | tf_op jit(solution)/shard_map/psum | solution.py:161
  271.2 2.0 copy-start.7
  271.2 7.0 %copy-start.16 = (bf16[1,16,128,256]{3,1,0,2:T(8,128)(2,1)S(1)}, bf16[1,16,128,256]{3,1,0,2:T(8,128)(2,1)}, u32[]{:S(2)}) copy-start(bf16[1,16,128,256]{3,1,0,2:T(8,128)(2,1)} %copy-done.15) | copy-start | bytes 3145732
  291.5 22.4 %copy-start.5 = (bf16[1,16,128,256]{2,3,1,0:T(8,128)(2,1)S(1)}, bf16[1,16,128,256]{2,3,1,0:T(8,128)(2,1)}, u32[]{:S(2)}) copy-start(bf16[1,16,128,256]{2,3,1,0:T(8,128)(2,1)} %copy.204) | copy-start | bytes 3145732
  325.5 2.6 copy-start.20
  364.4 102.8 %all-gather.6.cloned.1.call-start = ((), (), s32[]{:S(2)}) async-start(), calls=%async_computation.8 | async-start | bytes 2985984 | tf_op jit(solution)/shard_map/all_gather | solution.py:170
  365.0 110.5 %all-gather.8.cloned.1.call-start = ((), (), s32[]{:S(2)}) async-start(), calls=%async_computation.9 | async-start | bytes 2985984 | tf_op jit(solution)/shard_map/all_gather | solution.py:177
  365.6 174.9 %reduce-scatter.2.cloned.1.call-start = ((), (), s32[]{:S(2)}) async-start(), calls=%async_computation.10 | async-start | bytes 5898240 | tf_op jit(solution)/shard_map/reduce_scatter | solution.py:182
  461.9 2.1 copy-start.2
  461.9 2.1 copy-start.18
Sparse Core Ops, SparseCore 0:
  9.7 40.1 all-gather.3
  364.6 92.0 all-reduce.1
  494.0 46.4 reduce-scatter.1
Sparse Core Ops, SparseCore 1:
  367.1 52.9 all-gather.5
  422.1 53.4 all-gather.7
where the time goes:
time: 554 us; the launch traced here: 551 us
  waiting for transfers between devices  260 us (47%)
  local copies, waits for them, and re-layouts  89.8 us (16%)
  matrix products  89.8 us (16%)
  other arithmetic  47.2 us (9%)
  blocking collectives  30.6 us (6%)
  starting transfers between devices  17.9 us (3%)
  between operations  15.3 us (3%)
    psum x1, waiting for transfers between devices, shards(): lax.psum(partial_value.astype(jnp.bfloat16), 'mp').astype(jnp.float32)  91 us
    reduce_scatter x1, waiting for transfers between devices, shards(): lax.psum_scatter(downward.astype(jnp.bfloat16), 'mp', scatter_dimension=2...  46.6 us
    dot_general x2, matrix products, recurrence(): jnp.einsum('nhbqc,nhbsc->nhbqs', queries, weighted, precision=lax.Precisi...  44.5 us
    transpose x14, local copies, waits for them, and re-layouts, heads_first(): return shaped.transpose(0, 2, 1, 3)  42.1 us
    all_gather x1, waiting for transfers between devices, shards(): lax.all_gather(incoming_image_patches, 'mp', axis=2, tiled=True)  40.9 us
    all_to_all x1, blocking collectives, shards(): lax.all_to_all(back_grid, 'seq', split_axis=1, concat_axis=2, tiled=True)  30.6 us
    all_to_all x1, waiting for transfers between devices, shards(): lax.all_to_all(recept_grid, 'seq', split_axis=2, concat_axis=1, tiled=True)  24.2 us
    all_to_all x1, waiting for transfers between devices, shards(): lax.all_to_all(decay_grid, 'seq', split_axis=2, concat_axis=1, tiled=True)  24 us
  transfers between devices with their start and end apart: 9, of which 7 were waited for; matrix products, arithmetic and copies ran while one was open for 9% of the time, Pallas kernels for 0%

commit v1 on v0

--- a/solution.py
+++ b/solution.py
@@ -4,6 +4,7 @@
 from jax.sharding import PartitionSpec as P
 
 SUBSPACE_SIZE = 64
+create_slabs = lambda x_in: jnp.sum(lax.all_gather(x_in, axis_name="mp"), axis=0)
 
 
 def layer_norm(inputs, gain):
@@ -158,7 +159,7 @@
     )
     partial_value = lax.optimization_barrier(partial_value.astype(jnp.bfloat16)).astype(jnp.float32)
     partial_value = partial_value.reshape(images, row_count, full_cols, model_width)
-    totals = lax.psum(partial_value.astype(jnp.bfloat16), "mp").astype(jnp.float32)
+    totals = create_slabs(partial_value.astype(jnp.bfloat16)).astype(jnp.float32)
     residual_all = (whole_rows.astype(jnp.float32) + totals).astype(jnp.bfloat16)
     mix_input = layer_norm(residual_all, later_standardize_scaling)
     residual = lax.dynamic_slice_in_dim(

time: 554 us -> 672 us (1.21)
  waiting for transfers between devices: 260 us -> 366 us
  other arithmetic: 47.2 us -> 60.9 us
    all_gather x0 -> x1, waiting for transfers between devices: none -> 117 us  [lax.all_gather(x_in, axis_name='mp')]
    psum x1 -> x0, waiting for transfers between devices: 91 us -> none  [shards(): lax.psum(partial_value.astype(jnp.bfloat16), 'mp').astype(jnp.float32)]
    all_gather x1, waiting for transfers between devices: 0.01 us -> 55.6 us  [shards(): lax.all_gather(feature_mix_addressing_matrix, 'seq', axis=0, tiled=True)]
    all_gather x1, waiting for transfers between devices: 8.25 us -> 32.9 us  [shards(): lax.all_gather(feature_mix_content_matrix, 'seq', axis=1, tiled=True)]
    reduce_sum x0 -> x1, other arithmetic: none -> 13.9 us  [jnp.sum(lax.all_gather(x_in, axis_name='mp'), axis=0)]
  transfers between devices with their start and end apart: 9 -> 9, of which waited for: 7 -> 8; matrix products, arithmetic and copies ran while one was open for 9% -> 9% of each run, Pallas kernels for 0% -> 0%
where the time goes in v1:
time: 672 us; the launch traced here: 668 us
  waiting for transfers between devices  366 us (54%)
  matrix products  89.6 us (13%)
  local copies, waits for them, and re-layouts  89.1 us (13%)
  other arithmetic  60.9 us (9%)
  blocking collectives  30.6 us (5%)
  starting transfers between devices  17.8 us (3%)
  between operations  13.9 us (2%)
    all_gather x1, waiting for transfers between devices, lax.all_gather(x_in, axis_name='mp')  117 us
    all_gather x1, waiting for transfers between devices, shards(): lax.all_gather(feature_mix_addressing_matrix, 'seq', axis=0, tiled=True)  55.6 us
    reduce_scatter x1, waiting for transfers between devices, shards(): lax.psum_scatter(downward.astype(jnp.bfloat16), 'mp', scatter_dimension=2...  46.6 us
    dot_general x2, matrix products, recurrence(): jnp.einsum('nhbqc,nhbsc->nhbqs', queries, weighted, precision=lax.Precisi...  44.4 us
    transpose x14, local copies, waits for them, and re-layouts, heads_first(): return shaped.transpose(0, 2, 1, 3)  41.5 us
    all_gather x1, waiting for transfers between devices, shards(): lax.all_gather(incoming_image_patches, 'mp', axis=2, tiled=True)  40.9 us
    all_gather x1, waiting for transfers between devices, shards(): lax.all_gather(feature_mix_content_matrix, 'seq', axis=1, tiled=True)  32.9 us
    all_to_all x1, blocking collectives, shards(): lax.all_to_all(back_grid, 'seq', split_axis=1, concat_axis=2, tiled=True)  30.6 us
  transfers between devices with their start and end apart: 9, of which 8 were waited for; matrix products, arithmetic and copies ran while one was open for 9% of the time, Pallas kernels for 0%

profile of v1, /device:TPU:0, one launch (start us, length us, event | category | flops | bytes accessed | tf_op | source)
XLA Modules:
  0.0 668.4 jit_solution(6357435187911256981)
XLA Ops:
  8.2 40.9 %all-gather.5.cloned.1.call-done = bf16[1,16,128,1152]{3,2,1,0:T(8,128)(2,1)} async-done(((bf16[1,16,32,1152]{3,2,1,0:T(8,128)(2,1)}), bf16[1,16,128,1152]{3,2,1,0:T(8,128)(2,1)}) %all-gather.5.cloned.1.call-update) | async-done | bytes 4718608 | tf_op jit(solution)/shard_map/all_gather | solution.py:93
  49.1 3.2 convert_reduce_fusion
  56.4 2.1 copy-done.9
  60.1 3.2 reshape.314
  63.3 4.8 copy.216
  68.1 4.8 copy.187
  73.0 4.5 fusion.54
  77.5 3.2 reshape.315
  80.7 8.0 %bitcast_subtract_fusion = (f32[16,4,128,64]{3,0,1,2:T(8,128)S(1)}, f32[16,4,128,64]{3,0,1,2:T(8,128)}) fusion(f32[16,128,4,64]{3,2,1,0:T(4,128)} %reshape.315), kind=kOutput, calls=%fused_computation.42 | output fusion | flops 67108864 | bytes 6291456 | tf_op jit(solution)/shard_map/jit(cumsum)/reduce_window_sum | solution.py:34
  90.8 4.8 copy.196
  95.6 3.9 convolution_convert_fusion.3
  100.5 3.3 reshape.316
  103.7 3.5 copy.194
  107.2 5.7 convolution_convert_fusion.2
  113.0 2.3 copy.197
  116.7 22.1 %fusion.1 = f32[16,4,8,16,128]{4,3,2,1,0:T(8,128)S(1)} fusion(f32[16,4,128,64]{2,3,1,0:T(8,128)} %copy.196, f32[16,4,8,64]{3,2,1,0:T(8,128)S(1)} %copy.191, f32[16,4,128,64]{2,3,1,0:T(8,128)S(1)} %bitcast.139, pred[8,128]{1,0:T(8,128)(4,1)S(1)} %iota_compare_fusion.1, f32[16,4,8,16,64]{4,3,2,1,0:T(8,128)} %bitcast.165, f32[16,4,8,16,64]{4,0,1,3,2:T(8,128)} %bitcast.151), kind=kOutput, calls=%fused_computation.1 | convolution fusion | flops 818937856 | bytes 12715008 | tf_op jit(solution)/shard_map/nhbqc,nhbsc->nhbqs/dot_general | solution.py:47
  138.9 3.8 fusion.44
  142.6 3.5 copy.200
  146.2 2.9 fusion.57
  151.7 2.3 copy.201
  155.3 5.6 all-to-all-start.3
  161.0 2.9 copy.173
  163.8 23.4 %all-to-all-done.3 = bf16[1,16,128,256]{3,1,0,2:T(8,128)(2,1)} async-done(((bf16[1,16,128,256]{3,1,0,2:T(8,128)(2,1)}), bf16[1,16,128,256]{3,1,0,2:T(8,128)(2,1)}, u32[]{:S(2)}, u32[]{:S(2)}) %all-to-all-start.3) | async-done | bytes 1048608 | tf_op jit(solution)/shard_map/all_to_all | solution.py:133
  187.2 4.2 all-to-all-start.1
  193.1 24.0 %all-to-all-done.1 = bf16[1,16,128,256]{3,1,0,2:T(8,128)(2,1)} async-done(((bf16[1,16,128,256]{3,1,0,2:T(8,128)(2,1)}), bf16[1,16,128,256]{3,1,0,2:T(8,128)(2,1)}, u32[]{:S(2)}, u32[]{:S(2)}) %all-to-all-start.1) | async-done | bytes 1048608 | tf_op jit(solution)/shard_map/all_to_all | solution.py:132
  217.1 3.6 all-to-all-start
  222.2 24.2 %all-to-all-done = bf16[1,16,128,256]{3,1,0,2:T(8,128)(2,1)S(1)} async-done(((bf16[1,16,128,256]{3,1,0,2:T(8,128)(2,1)}), bf16[1,16,128,256]{3,1,0,2:T(8,128)(2,1)S(1)}, u32[]{:S(2)}, u32[]{:S(2)}) %all-to-all-start) | async-done | bytes 1048608 | tf_op jit(solution)/shard_map/all_to_all | solution.py:130
  246.5 4.2 all-to-all-start.2
  259.5 4.5 copy.177
  264.0 6.1 bitcast_subtract_fusion.1
  272.2 4.7 copy.185
  281.1 2.7 copy.172
  287.1 3.0 copy.183
  290.1 22.3 %fusion.6 = f32[16,4,8,16,128]{4,3,2,1,0:T(8,128)S(1)} fusion(f32[16,4,128,64]{2,3,1,0:T(8,128)} %copy.185, f32[16,4,8,64]{3,2,1,0:T(8,128)S(1)} %copy.178, f32[16,4,128,64]{2,3,1,0:T(8,128)} %bitcast.144, pred[8,128]{1,0:T(8,128)(4,1)S(1)} %iota_compare_fusion.1, f32[16,4,8,16,64]{4,3,2,1,0:T(8,128)} %bitcast.164, f32[16,4,8,16,64]{4,0,1,3,2:T(8,128)} %bitcast.149), kind=kOutput, calls=%fused_computation.6 | convolution fusion | flops 818937856 | bytes 12715008 | tf_op jit(solution)/shard_map/nhbqc,nhbsc->nhbqs/dot_general | solution.py:47
  312.4 3.7 fusion.46
  316.1 4.0 copy.205
  320.1 3.2 fusion.80
  328.2 30.6 %all_to_all.69 = bf16[1,128,16,256]{3,2,0,1:T(8,128)(2,1)S(1)} all-to-all(bf16[1,128,16,256]{3,2,0,1:T(8,128)(2,1)S(1)} %fusion.68), channel_id=1, replica_groups=mesh['seq'=8,'mp'=4] {'seq'}, dimensions={1} | all-to-all | bytes 2097152 | tf_op jit(solution)/shard_map/all_to_all | solution.py:154
  359.0 3.7 convolution_convert_fusion.1
  364.1 116.8 %all-gather.7.cloned.1.call-done = bf16[4,1,16,128,1152]{4,3,2,1,0:T(8,128)(2,1)} async-done(((bf16[1,1,16,128,1152]{4,3,2,1,0:T(8,128)(2,1)}), bf16[4,1,16,128,1152]{4,3,2,1,0:T(8,128)(2,1)}) %all-gather.7.cloned.1.call-update) | async-done | bytes 18874384 | tf_op jit(solution)/shard_map/all_gather | solution.py:7
  480.9 13.9 %reduce_sum.110 = bf16[16,128,1152]{2,1,0:T(8,128)(2,1)} reduce(bf16[4,1,16,128,1152]{4,3,2,1,0:T(8,128)(2,1)} %all-gather.7.cloned.1.call-done, bf16[]{:T(256)} %constant.41.clone.1), dimensions={0,1}, to_apply=%region_10.11 | reduce | flops 7077888 | bytes 23592962 | tf_op jit(solution)/shard_map/reduce_sum | solution.py:7
  494.8 5.3 convert_reduce_fusion.1
  502.2 3.0 fusion.21
  505.2 32.9 %all-gather.11.cloned.1.call-done = bf16[1152,1152]{0,1:T(8,128)(2,1)} async-done(((bf16[1152,144]{0,1:T(8,128)(2,1)}), bf16[1152,1152]{0,1:T(8,128)(2,1)}) %all-gather.11.cloned.1.call-update) | async-done | bytes 2654224 | tf_op jit(solution)/shard_map/all_gather | solution.py:178
  538.1 55.6 %all-gather.9.cloned.1.call-done = bf16[1152,1152]{1,0:T(8,128)(2,1)} async-done(((bf16[144,1152]{1,0:T(8,128)(2,1)}), bf16[1152,1152]{1,0:T(8,128)(2,1)}) %all-gather.9.cloned.1.call-update) | async-done | bytes 2654224 | tf_op jit(solution)/shard_map/all_gather | solution.py:171
  593.7 18.4 %convolution_convert_fusion = bf16[2048,1152]{1,0:T(8,128)(2,1)} fusion(bf16[1152,1152]{0,1:T(8,128)(2,1)} %all-gather.11.cloned.1.call-done, bf16[2048,1152]{1,0:T(8,128)(2,1)} %bitcast.157, bf16[1152,1152]{1,0:T(8,128)(2,1)} %all-gather.9.cloned.1.call-done), kind=kOutput, calls=%fused_computation.40 | convolution fusion | flops 10881073152 | bytes 14745600 | tf_op jit(solution)/shard_map/dot_general | solution.py:176
  612.1 46.6 %reduce-scatter.2.cloned.1.call-done = bf16[1,16,32,1152]{3,2,1,0:T(8,128)(2,1)} async-done(((bf16[1,16,128,1152]{3,2,1,0:T(8,128)(2,1)}), bf16[1,16,32,1152]{3,2,1,0:T(8,128)(2,1)}) %reduce-scatter.2.cloned.1.call-update) | async-done | bytes 1179664 | tf_op jit(solution)/shard_map/reduce_scatter | solution.py:183
  658.7 2.9 add_convert_fusion
  (112 shorter events, 45.7 us)
Async XLA Ops:
  6.5 352.4 %copy-start = (bf16[256,1152]{1,0:T(8,128)(2,1)S(1)}, bf16[256,1152]{1,0:T(8,128)(2,1)}, u32[]{:S(2)}) copy-start(bf16[256,1152]{1,0:T(8,128)(2,1)} %param.26) | copy-start | bytes 1769476
  6.5 42.5 %all-gather.5.cloned.1.call-start = ((), (), s32[]{:S(2)}) async-start(), calls=%async_computation.6 | async-start | bytes 5898240 | tf_op jit(solution)/shard_map/all_gather | solution.py:93
  8.2 46.1 %copy-start.17 = (f32[1152]{0:T(1024)S(1)}, f32[1152]{0:T(1024)}, u32[]{:S(2)}) copy-start(f32[1152]{0:T(1024)} %param.16) | copy-start | bytes 13828
  49.1 3.8 copy-start.1
  54.3 4.2 copy-start.21
  56.4 2.1 copy-start.9
  60.1 8.0 %copy-start.10 = (bf16[2048,256]{1,0:T(8,128)(2,1)}, bf16[2048,256]{1,0:T(8,128)(2,1)S(1)}, u32[]{:S(2)}) copy-start(bf16[2048,256]{1,0:T(8,128)(2,1)S(1)} %convolution_convert_fusion.4) | copy-start | bytes 3145732
  68.1 4.8 copy-start.23
  68.1 4.8 copy-start.24
  68.1 4.8 copy-start.25
  77.4 11.2 %copy-start.14 = (bf16[2048,256]{1,0:T(8,128)(2,1)}, bf16[2048,256]{1,0:T(8,128)(2,1)S(1)}, u32[]{:S(2)}) copy-start(bf16[2048,256]{1,0:T(8,128)(2,1)S(1)} %fusion.54) | copy-start | bytes 3145732
  88.6 2.0 copy-start.8
  88.6 7.0 %copy-start.22 = (bf16[1152,256]{1,0:T(8,128)(2,1)S(1)}, bf16[1152,256]{1,0:T(8,128)(2,1)}, u32[]{:S(2)}) copy-start(bf16[1152,256]{1,0:T(8,128)(2,1)} %param.18) | copy-start | bytes 1769476
  99.4 1.0 copy-start.12
  107.2 9.5 %copy-start.6 = (f32[16,128,4,64]{1,3,2,0:T(8,128)}, f32[16,128,4,64]{1,3,2,0:T(8,128)S(1)}, u32[]{:S(2)}) copy-start(f32[16,128,4,64]{1,3,2,0:T(8,128)S(1)} %copy.194) | copy-start | bytes 6291460
  116.7 22.1 %copy-start.3 = (bf16[32,8,16,128]{3,2,1,0:T(8,128)(2,1)}, bf16[32,8,16,128]{3,2,1,0:T(8,128)(2,1)S(1)}, u32[]{:S(2)}) copy-start(bf16[32,8,16,128]{3,2,1,0:T(8,128)(2,1)S(1)} %copy.223) | copy-start | bytes 3145732
  146.1 2.9 copy-start.4
  149.9 4.1 copy-start.19
  155.3 36.2 %copy-start.11 = (bf16[2048,256]{1,0:T(8,128)(2,1)S(1)}, bf16[2048,256]{1,0:T(8,128)(2,1)}, u32[]{:S(2)}) copy-start(bf16[2048,256]{1,0:T(8,128)(2,1)} %copy-done.10) | copy-start | bytes 3145732
  155.3 31.9 %all-to-all-start.3 = ((bf16[1,16,128,256]{3,1,0,2:T(8,128)(2,1)}), bf16[1,16,128,256]{3,1,0,2:T(8,128)(2,1)}, u32[]{:S(2)}, u32[]{:S(2)}) async-start(bf16[1,16,128,256]{3,1,0,2:T(8,128)(2,1)} %multiply_convert_fusion.1), calls=%async_computation.3 | async-start | bytes 2097152 | tf_op jit(solution)/shard_map/all_to_all | solution.py:133
  161.0 59.7 %copy-start.13 = (bf16[2048,256]{1,0:T(8,128)(2,1)S(1)}, bf16[2048,256]{1,0:T(8,128)(2,1)}, u32[]{:S(2)}) copy-start(bf16[2048,256]{1,0:T(8,128)(2,1)} %copy-done.12) | copy-start | bytes 3145732
  187.2 29.8 %all-to-all-start.1 = ((bf16[1,16,128,256]{3,1,0,2:T(8,128)(2,1)}), bf16[1,16,128,256]{3,1,0,2:T(8,128)(2,1)}, u32[]{:S(2)}, u32[]{:S(2)}) async-start(bf16[1,16,128,256]{3,1,0,2:T(8,128)(2,1)} %copy.173), calls=%async_computation.1 | async-start | bytes 2097152 | tf_op jit(solution)/shard_map/all_to_all | solution.py:132
  217.1 29.4 %all-to-all-start = ((bf16[1,16,128,256]{3,1,0,2:T(8,128)(2,1)}), bf16[1,16,128,256]{3,1,0,2:T(8,128)(2,1)S(1)}, u32[]{:S(2)}, u32[]{:S(2)}) async-start(bf16[1,16,128,256]{3,1,0,2:T(8,128)(2,1)} %copy.168), calls=%async_computation | async-start | bytes 2097152 | tf_op jit(solution)/shard_map/all_to_all | solution.py:130
  246.5 7.7 %copy-start.15 = (bf16[1,16,128,256]{3,1,0,2:T(8,128)(2,1)}, bf16[1,16,128,256]{3,1,0,2:T(8,128)(2,1)S(1)}, u32[]{:S(2)}) copy-start(bf16[1,16,128,256]{3,1,0,2:T(8,128)(2,1)S(1)} %all-to-all-done) | copy-start | bytes 3145732
  246.5 37.3 %all-to-all-start.2 = ((bf16[1,16,128,256]{3,1,0,2:T(8,128)(2,1)}), bf16[1,16,128,256]{3,1,0,2:T(8,128)(2,1)}, u32[]{:S(2)}, u32[]{:S(2)}) async-start(bf16[1,16,128,256]{3,1,0,2:T(8,128)(2,1)} %copy.180), calls=%async_computation.2 | async-start | bytes 2097152 | tf_op jit(solution)/shard_map/all_to_all | solution.py:131
  250.7 230.2 %all-gather.7.cloned.1.call-start = ((), (), s32[]{:S(2)}) async-start(), calls=%async_computation.7 | async-start | bytes 23592960 | tf_op jit(solution)/shard_map/all_gather | solution.py:7
  270.1 2.0 copy-start.7
  270.1 6.9 %copy-start.16 = (bf16[1,16,128,256]{3,1,0,2:T(8,128)(2,1)S(1)}, bf16[1,16,128,256]{3,1,0,2:T(8,128)(2,1)}, u32[]{:S(2)}) copy-start(bf16[1,16,128,256]{3,1,0,2:T(8,128)(2,1)} %copy-done.15) | copy-start | bytes 3145732
  290.1 22.3 %copy-start.5 = (bf16[1,16,128,256]{2,3,1,0:T(8,128)(2,1)S(1)}, bf16[1,16,128,256]{2,3,1,0:T(8,128)(2,1)}, u32[]{:S(2)}) copy-start(bf16[1,16,128,256]{2,3,1,0:T(8,128)(2,1)} %copy.204) | copy-start | bytes 3145732
  323.9 2.5 copy-start.20
  362.7 175.4 %all-gather.11.cloned.1.call-start = ((), (), s32[]{:S(2)}) async-start(), calls=%async_computation.9 | async-start | bytes 2985984 | tf_op jit(solution)/shard_map/all_gather | solution.py:178
  363.5 230.2 %all-gather.9.cloned.1.call-start = ((), (), s32[]{:S(2)}) async-start(), calls=%async_computation.8 | async-start | bytes 2985984 | tf_op jit(solution)/shard_map/all_gather | solution.py:171
  364.0 294.7 %reduce-scatter.2.cloned.1.call-start = ((), (), s32[]{:S(2)}) async-start(), calls=%async_computation.10 | async-start | bytes 5898240 | tf_op jit(solution)/shard_map/reduce_scatter | solution.py:183
  500.0 2.1 copy-start.2
  500.0 2.1 copy-start.18
Sparse Core Ops, SparseCore 0:
  8.9 40.1 all-gather.4
  362.8 118.0 all-gather.6
  483.1 54.9 all-gather.10
  540.1 53.5 all-gather.8
  612.2 46.4 reduce-scatter.1
